TPU v7x, 512 devices: a whole 4x8x8 slice. The times are simulated.
512 devices in a mesh: pp: 8 (over x, z_lo), ep: 64 (over y, z_hi, core).
Axes of the slice: x: 4, y: 8, z: 8 (z_hi: 4, z_lo: 2; z = z_hi * 2 + z_lo), core: 2. Of those that a mesh axis runs over, the one named last changes fastest.
Arguments:
- fwd_act: bfloat16 [8, 4096, 3584], P('pp', 'ep'), may hold values from -6 to 6
- fwd_route: int32 [8, 4096, 1], P('pp', 'ep'), may hold values from 0 to 7, as said below
- fwd_gate: float32 [8, 4096, 1], P('pp', 'ep'), may hold values from 0.25 to 2
- bwd_act: bfloat16 [8, 4096, 3584], P('pp', 'ep'), may hold values from -6 to 6
- bwd_grad: bfloat16 [8, 4096, 3584], P('pp', 'ep'), may hold values from -6 to 6
- bwd_route: int32 [8, 4096, 1], P('pp', 'ep'), may hold values from 0 to 7, as said below
- bwd_gate: float32 [8, 4096, 1], P('pp', 'ep'), may hold values from 0.25 to 2
- norm_gain: float32 [8, 3584], P('pp'), may hold values from 0.25 to 1.75
- w_gate: bfloat16 [8, 64, 1792, 256], P('pp', 'ep'), may hold values from -0.09375 to 0.09375
- w_up: bfloat16 [8, 64, 1792, 256], P('pp', 'ep'), may hold values from -0.09375 to 0.09375
- w_down: bfloat16 [8, 64, 256, 1792], P('pp', 'ep'), may hold values from -0.1875 to 0.1875
Outputs:
- fwd_next: bfloat16 [8, 4096, 3584], P('pp', 'ep')
- bwd_next: bfloat16 [8, 4096, 3584], P('pp', 'ep')
Inputs may be any that keep to these rules, and one draw needn't show every extreme that they name: `fwd_route`: among the 64 rows of one device, no expert is named more than 10 times; at each section one expert is named exactly 10 times in every device's rows. `bwd_route`: as fwd_route, drawn independently.
All inputs are finite; a program needn't handle non-finite values.
Results may differ from a plain program's by a relative error of at most 0.011.
Values may be sent and summed in bfloat16 or wider, within the bound.
A program may use at most 128 MiB of HBM per device.

v0:
```python
import jax
import jax.numpy as jnp
from jax import lax
from jax.sharding import Mesh
from jax.sharding import PartitionSpec as P

SLICES = 8
EP = ("ep_0", "ep_1", "ep_2")


def from_partner(value, axis, stride):
    return lax.ppermute(value, axis, [(i, i ^ 1 << stride) for i in range(lax.axis_size(axis))])


def in_blocks(value, dim, size):
    before, after = (value.shape[:dim], value.shape[dim + 1 :])
    return jnp.moveaxis(value.reshape(*before, size, -1, *after), dim, 0)


def laid_out(blocks, dim):
    blocks = jnp.moveaxis(blocks, 0, dim)
    lengths = blocks.shape
    return blocks.reshape(*lengths[:dim], lengths[dim] * lengths[dim + 1], *lengths[dim + 2 :])


def exchange_in_order(blocks, axes, sequence):
    inside = blocks.shape[1:]
    result = blocks.reshape(*(lax.axis_size(a) for a in axes), *inside)
    for k in sequence:
        result = lax.all_to_all(result, axes[k], k, k, tiled=True)
    return result.reshape(-1, *inside)


def core_and_chips(value, groups, sequence, split_dim, concat_dim):
    size = lax.axis_size(groups[0]) * lax.axis_size(groups[1])
    blocks = in_blocks(value, split_dim, size)
    return laid_out(exchange_in_order(blocks, groups, sequence), concat_dim)


def from_behind(value, axis, steps):
    count = lax.axis_size(axis)
    pairs = [(source, (source + steps) % count) for source in range(count)]
    return lax.ppermute(value, axis, pairs)


def normalize(values, norm_scale):
    widened = values.astype(jnp.float32)
    inverse = lax.rsqrt(jnp.mean(widened * widened, axis=-1, keepdims=True) + 1e-06)
    return ((widened * inverse * norm_scale).astype(jnp.bfloat16), inverse)


def slot_plan(route_ids, experts, capacity):
    chosen = route_ids[:, 0]
    onehot = (chosen[:, None] == jnp.arange(experts, dtype=jnp.int32)[None, :]).astype(jnp.int32)
    running = jnp.cumsum(onehot, axis=0) - 1
    position = jnp.sum(running * onehot, axis=1)
    target = chosen * capacity + position
    chooser = (jnp.arange(experts * capacity, dtype=jnp.int32)[:, None] == target[None, :]).astype(
        jnp.bfloat16
    )
    return (target, chooser)


def lay_out(chooser, members, experts, capacity):
    half_width = members[0].shape[1] // 2
    pieces = []
    for half in range(2):
        for member in members:
            columns = member[:, half * half_width : (half + 1) * half_width]
            placed = jnp.dot(chooser, columns, preferred_element_type=jnp.float32).astype(
                jnp.bfloat16
            )
            pieces.append(placed.reshape(experts, capacity * half_width))
    stacked = jnp.stack(pieces, axis=1)
    return stacked.reshape(experts, 2, len(members) * capacity * half_width)


def send_rows(placed, count, capacity, half_width):
    experts = placed.shape[0]
    blocks = SLICES // 2
    length = placed.shape[2]
    half_slots = capacity // 2
    shaped = placed.reshape(experts, 2, count, capacity, half_width)
    pieces = [
        shaped[
            :, :, :, hidden_block % 2 * half_slots : (hidden_block % 2 + 1) * half_slots
        ].reshape(experts, 2, length // 2)
        for hidden_block in range(blocks)
    ]
    outgoing = jnp.stack(pieces, axis=1).reshape(-1, length // 2)
    arrived = lax.all_to_all(outgoing, EP, split_axis=0, concat_axis=0, tiled=True)
    partner = from_partner(arrived, EP, 1)
    odd_block = lax.axis_index(EP) // 2 % 2 == 1
    lower_part = jnp.where(odd_block, partner, arrived).reshape(-1, count, half_slots, half_width)
    upper_part = jnp.where(odd_block, arrived, partner).reshape(-1, count, half_slots, half_width)
    return jnp.concatenate([lower_part, upper_part], axis=2).reshape(-1, length)


def member_rows(arrived, member, count, half_width):
    senders = arrived.shape[0]
    return arrived.reshape(senders, count, -1)[:, member].reshape(-1, half_width)


def pair_sum(stacked):
    return stacked + from_partner(stacked.astype(jnp.bfloat16), EP, 0).astype(stacked.dtype)


def return_rows(results):
    return core_and_chips(results, (("ep_0", "ep_1"), "ep_2"), (1, 0), 0, 0)


def gather_back(returned, target, experts, capacity, half_width):
    summed = (
        returned.reshape(experts, SLICES // 2, 2, capacity * half_width)
        .astype(jnp.float32)
        .sum(axis=1)
    )
    halves = [
        jnp.take(summed[:, half].reshape(experts * capacity, half_width), target, axis=0)
        for half in range(2)
    ]
    return jnp.concatenate(halves, axis=1)


def body(
    fwd_act,
    fwd_route,
    fwd_gate,
    bwd_act,
    bwd_grad,
    bwd_route,
    bwd_gate,
    norm_gain,
    w_gate,
    w_up,
    w_down,
):
    senders = lax.axis_size(EP)
    experts = senders // SLICES
    tokens_here = fwd_act.shape[1]
    capacity = 2 * ((5 * tokens_here + 8 * experts - 1) // (8 * experts))
    norm_scale = norm_gain[0]
    gate_weight = w_gate[0, 0]
    up_weight = w_up[0, 0]
    down_weight = w_down[0, 0]
    half_width = gate_weight.shape[0]
    contract = (((1,), (1,)), ((), ()))
    fwd_rows = fwd_act[0]
    fwd_normed, fwd_inverse = normalize(fwd_rows, norm_scale)
    fwd_target, fwd_chooser = slot_plan(fwd_route[0], experts, capacity)
    fwd_arrived = send_rows(
        lay_out(fwd_chooser, (fwd_normed,), experts, capacity), 1, capacity, half_width
    )
    fwd_inputs = member_rows(fwd_arrived, 0, 1, half_width)
    fwd_pre = pair_sum(
        jnp.stack(
            [
                jnp.dot(fwd_inputs, gate_weight, preferred_element_type=jnp.float32),
                jnp.dot(fwd_inputs, up_weight, preferred_element_type=jnp.float32),
            ]
        )
    )
    hidden = (jax.nn.silu(fwd_pre[0]) * fwd_pre[1]).astype(jnp.bfloat16)
    fwd_partial = jnp.dot(hidden, down_weight, preferred_element_type=jnp.float32).astype(
        jnp.bfloat16
    )
    fwd_returned = return_rows(fwd_partial.reshape(senders, capacity * half_width))
    fwd_mixed = gather_back(fwd_returned, fwd_target, experts, capacity, half_width)
    fwd_result = (fwd_rows.astype(jnp.float32) + fwd_gate[0] * fwd_mixed).astype(jnp.bfloat16)
    fwd_next = from_behind(fwd_result, "pp", 1)
    bwd_rows = bwd_act[0]
    bwd_normed, bwd_inverse = normalize(bwd_rows, norm_scale)
    weighted = (bwd_gate[0] * bwd_grad[0].astype(jnp.float32)).astype(jnp.bfloat16)
    bwd_target, bwd_chooser = slot_plan(bwd_route[0], experts, capacity)
    bwd_arrived = send_rows(
        lay_out(bwd_chooser, (bwd_normed, weighted), experts, capacity), 2, capacity, half_width
    )
    bwd_inputs = member_rows(bwd_arrived, 0, 2, half_width)
    grad_inputs = member_rows(bwd_arrived, 1, 2, half_width)
    bwd_pre = pair_sum(
        jnp.stack(
            [
                jnp.dot(bwd_inputs, gate_weight, preferred_element_type=jnp.float32),
                jnp.dot(bwd_inputs, up_weight, preferred_element_type=jnp.float32),
                lax.dot_general(
                    grad_inputs, down_weight, contract, preferred_element_type=jnp.float32
                ),
            ]
        )
    )
    logistic = jax.nn.sigmoid(bwd_pre[0])
    d_gate = (bwd_pre[2] * bwd_pre[1] * logistic * (1.0 + bwd_pre[0] * (1.0 - logistic))).astype(
        jnp.bfloat16
    )
    d_up = (bwd_pre[2] * bwd_pre[0] * logistic).astype(jnp.bfloat16)
    d_partial = (
        lax.dot_general(d_gate, gate_weight, contract, preferred_element_type=jnp.float32)
        + lax.dot_general(d_up, up_weight, contract, preferred_element_type=jnp.float32)
    ).astype(jnp.bfloat16)
    bwd_returned = return_rows(d_partial.reshape(senders, capacity * half_width))
    d_normed = gather_back(bwd_returned, bwd_target, experts, capacity, half_width)
    scaled = norm_scale * d_normed
    widened = bwd_rows.astype(jnp.float32)
    cubed = bwd_inverse * bwd_inverse * bwd_inverse
    d_rows = (
        bwd_grad[0].astype(jnp.float32)
        + scaled * bwd_inverse
        - widened * cubed * jnp.mean(scaled * widened, axis=-1, keepdims=True)
    )
    bwd_next = from_behind(d_rows.astype(jnp.bfloat16), "pp", -1)
    return (fwd_next[None], bwd_next[None])


def solution(mesh):
    split = Mesh(mesh.devices.reshape(mesh.shape["pp"], 8, 4, 2), ("pp", "ep_0", "ep_1", "ep_2"))
    return jax.shard_map(
        body,
        mesh=split,
        in_specs=(
            P("pp", EP, None),
            P("pp", EP, None),
            P("pp", EP, None),
            P("pp", EP, None),
            P("pp", EP, None),
            P("pp", EP, None),
            P("pp", EP, None),
            P("pp", None),
            P("pp", EP, None, None),
            P("pp", EP, None, None),
            P("pp", EP, None, None),
        ),
        out_specs=(P("pp", EP, None), P("pp", EP, None)),
        check_vma=False,
    )
```

profile of v0, /device:TPU:1, one launch (start us, length us, event | category | flops | bytes accessed | tf_op | source)
XLA Modules:
  0.0 720.3 jit_solution(1697948917369257349)
XLA Ops:
  11.7 1.9 reshape_reshape.7
  19.1 6.7 all_to_all.39
  26.3 45.2 %reduce.13 = bf16[64,17920]{1,0:T(8,128)(2,1)S(1)} reduce(bf16[64,1,17920]{2,1,0:T(2,128)(2,1)} %all_to_all.39, bf16[]{:T(256)} %broadcast.117), dimensions={1}, to_apply=%all_to_all.39.reduce_sub_computation | reduce | bytes 4587522 | tf_op jit(solution)/shard_map/all_to_all | solution.py:91
  71.5 2.1 reshape.157
  73.6 77.4 %all_to_all.46 = bf16[64,2,8960]{2,1,0:T(2,128)(2,1)S(1)} all-to-all(bf16[64,2,8960]{2,1,0:T(2,128)(2,1)} %reshape.157), channel_id=1, replica_groups=mesh['pp'=8,'ep_0'=8,'ep_1'=4,'ep_2'=2] {'ep_0','ep_1','ep_2'}, dimensions={0} | all-to-all | bytes 4587520 | tf_op jit(solution)/shard_map/all_to_all | solution.py:91
  151.1 6.7 reshape.158
  157.7 2.6 copy.53
  160.3 2.5 collective-permute-start.3
  162.9 100.5 %collective-permute-done.3 = bf16[64,17920]{1,0:T(8,128)(2,1)} collective-permute-done((bf16[64,17920]{1,0:T(8,128)(2,1)S(1)}, bf16[64,17920]{1,0:T(8,128)(2,1)}, u32[]{:S(2)}, u32[]{:S(2)}) %collective-permute-start.3) | collective-permute-done | bytes 2293792 | tf_op jit(solution)/shard_map/ppermute | solution.py:12
  263.4 4.8 broadcast_select_fusion.1
  268.2 6.3 reshape.95
  274.5 4.5 reshape.96
  279.0 8.9 %pad_maximum_fusion = bf16[64,2,10,1792]{3,2,1,0:T(8,128)(2,1)} fusion(bf16[64,2,5,1792]{3,2,1,0:T(8,128)(2,1)} %reshape.96, bf16[64,2,5,1792]{3,2,1,0:T(8,128)(2,1)} %reshape.95), kind=kLoop, calls=%fused_computation.4 | loop fusion | flops 9175040 | bytes 9175040 | tf_op jit(solution)/shard_map/concatenate | solution.py:96
  287.9 13.0 %reshape.146 = bf16[64,2,17920]{2,1,0:T(2,128)(2,1)} reshape(bf16[64,2,10,1792]{3,2,1,0:T(8,128)(2,1)} %pad_maximum_fusion) | data formatting | bytes 9175040 | tf_op jit(solution)/shard_map/reshape;reshape | solution.py:101
  300.9 52.5 %slice_reduce_fusion.1 = (bf16[64,17920]{1,0:T(8,128)(2,1)S(1)}, bf16[64,17920]{1,0:T(8,128)(2,1)}) fusion(bf16[64,2,17920]{2,1,0:T(2,128)(2,1)} %reshape.146), kind=kLoop, calls=%fused_computation.6 | loop fusion | bytes 9175040 | tf_op jit(solution)/shard_map/slice | solution.py:101
  353.5 5.9 reshape_squeeze.21
  359.4 4.5 reshape_squeeze.20
  363.8 2.6 convolution_bitcast_fusion.1
  369.3 3.1 collective-permute-start.4
  372.4 2.2 collective-permute-done.4
  376.6 2.2 reshape_reshape_reshape.9
  380.7 5.6 all_to_all.47
  386.3 3.7 copy.41
  390.0 4.8 all-to-all-start.5
  395.3 58.1 %all-to-all-done.5 = bf16[32,2,1,17920]{3,1,2,0:T(2,128)(2,1)S(1)} async-done(((bf16[32,2,1,17920]{3,1,2,0:T(2,128)(2,1)}), bf16[32,2,1,17920]{3,1,2,0:T(2,128)(2,1)S(1)}, u32[]{:S(2)}, u32[]{:S(2)}) %all-to-all-start.5) | async-done | bytes 2293792 | tf_op jit(solution)/shard_map/all_to_all | solution.py:30
  453.4 2.2 convert_reduce_fusion
  455.7 2.9 slice_reduce_fusion.3
  466.7 4.5 all_to_all.38
  471.2 8.6 %reduce.14 = bf16[64,8960]{1,0:T(8,128)(2,1)} reduce(bf16[64,1,8960]{2,1,0:T(2,128)(2,1)S(1)} %all_to_all.38, bf16[]{:T(256)} %broadcast.117), dimensions={1}, to_apply=%all_to_all.38.reduce_sub_computation | reduce | bytes 2293762 | tf_op jit(solution)/shard_map/all_to_all | solution.py:91
  481.1 50.8 %all_to_all.48 = bf16[64,2,4480]{2,1,0:T(2,128)(2,1)} all-to-all(bf16[64,2,4480]{2,1,0:T(2,128)(2,1)S(1)} %reshape.155), channel_id=1, replica_groups=mesh['pp'=8,'ep_0'=8,'ep_1'=4,'ep_2'=2] {'ep_0','ep_1','ep_2'}, dimensions={0} | all-to-all | bytes 2293760 | tf_op jit(solution)/shard_map/all_to_all | solution.py:91
  531.9 6.6 reshape.156
  538.7 4.6 collective-permute-start
  543.2 50.2 %collective-permute-done = bf16[64,8960]{1,0:T(8,128)(2,1)S(1)} collective-permute-done((bf16[64,8960]{1,0:T(8,128)(2,1)S(1)}, bf16[64,8960]{1,0:T(8,128)(2,1)S(1)}, u32[]{:S(2)}, u32[]{:S(2)}) %collective-permute-start) | collective-permute-done | bytes 1146912 | tf_op jit(solution)/shard_map/ppermute | solution.py:12
  595.1 3.3 reshape.93
  598.4 4.1 reshape.94
  602.5 4.5 pad_maximum_fusion.1
  607.1 3.9 reshape_squeeze_reshape_reshape.3
  613.0 2.6 collective-permute-start.1
  617.5 2.2 convolution_convert_fusion
  619.7 2.7 reshape_reshape_reshape.8
  622.7 5.6 all_to_all.49
  628.3 3.7 copy.34
  632.0 6.1 all-to-all-start.2
  638.1 4.2 collective-permute-start.5
  642.3 55.0 %all-to-all-done.2 = bf16[32,2,1,17920]{3,1,2,0:T(2,128)(2,1)S(1)} async-done(((bf16[32,2,1,17920]{3,1,2,0:T(2,128)(2,1)}), bf16[32,2,1,17920]{3,1,2,0:T(2,128)(2,1)S(1)}, u32[]{:S(2)}, u32[]{:S(2)}) %all-to-all-start.2) | async-done | bytes 2293792 | tf_op jit(solution)/shard_map/all_to_all | solution.py:30
  697.2 2.2 convert_reduce_fusion.1
  699.5 2.9 slice_reduce_fusion.5
  706.5 10.6 %collective-permute-done.2 = bf16[64,3584]{1,0:T(8,128)(2,1)S(1)} collective-permute-done((bf16[64,3584]{1,0:T(8,128)(2,1)S(1)}, bf16[64,3584]{1,0:T(8,128)(2,1)S(1)}, u32[]{:S(2)}, u32[]{:S(2)}) %collective-permute-start.2) | collective-permute-done | bytes 458784 | tf_op jit(solution)/shard_map/ppermute | solution.py:43
  (111 shorter events, 45.8 us)
Async XLA Ops:
  0.6 363.2 %copy-start = (bf16[1,1,1792,256]{3,2,1,0:T(8,128)(2,1)S(1)}, bf16[1,1,1792,256]{3,2,1,0:T(8,128)(2,1)}, u32[]{:S(2)}) copy-start(bf16[1,1,1792,256]{3,2,1,0:T(8,128)(2,1)} %param.22) | copy-start | bytes 2752516
  0.6 7.3 %copy-start.12 = (f32[1,64,1]{1,2,0:T(1,128)S(1)}, f32[1,64,1]{1,2,0:T(1,128)}, u32[]{:S(2)}) copy-start(f32[1,64,1]{1,2,0:T(1,128)} %param.19) | copy-start | bytes 772
  0.7 7.3 %copy-start.7 = (bf16[1,64,3584]{2,1,0:T(8,128)(2,1)S(1)}, bf16[1,64,3584]{2,1,0:T(8,128)(2,1)}, u32[]{:S(2)}) copy-start(bf16[1,64,3584]{2,1,0:T(8,128)(2,1)} %param.17) | copy-start | bytes 1376260
  14.9 1.2 copy-start.4
  160.3 103.1 %collective-permute-start.3 = (bf16[64,17920]{1,0:T(8,128)(2,1)S(1)}, bf16[64,17920]{1,0:T(8,128)(2,1)}, u32[]{:S(2)}, u32[]{:S(2)}) collective-permute-start(bf16[64,17920]{1,0:T(8,128)(2,1)S(1)} %bitcast.96), channel_id=1, source_target_pairs={{0,2},{1,3},{2,0},{3,1},{4,6},{5,7},{6,4},{7,5},{8,10},{9,11},{10,... | collective-permute-start | bytes 6881288 | tf_op jit(solution)/shard_map/ppermute | solution.py:12
  363.8 2.6 copy-start.6
  363.8 2.6 copy-start.9
  366.4 1.6 copy-start.5
  366.4 1.9 copy-start.14
  369.3 5.3 collective-permute-start.4
  390.0 4.9 copy-start.11
  390.0 63.4 %all-to-all-start.5 = ((bf16[32,2,1,17920]{3,1,2,0:T(2,128)(2,1)}), bf16[32,2,1,17920]{3,1,2,0:T(2,128)(2,1)S(1)}, u32[]{:S(2)}, u32[]{:S(2)}) async-start(bf16[32,2,1,17920]{3,1,2,0:T(2,128)(2,1)} %copy.41), calls=%async_computation.5 | async-start | bytes 4587520 | tf_op jit(solution)/shard_map/all_to_all | solution.py:30
  459.6 1.0 copy-start.1
  460.4 1.1 copy-start.2
  460.4 1.2 copy-start.8
  538.7 54.8 %collective-permute-start = (bf16[64,8960]{1,0:T(8,128)(2,1)S(1)}, bf16[64,8960]{1,0:T(8,128)(2,1)S(1)}, u32[]{:S(2)}, u32[]{:S(2)}) collective-permute-start(bf16[64,8960]{1,0:T(8,128)(2,1)S(1)} %bitcast.97), channel_id=1, source_target_pairs={{0,2},{1,3},{2,0},{3,1},{4,6},{5,7},{6,4},{7,5},{8,10},{9,11},{10,... | collective-permute-start | bytes 3440648 | tf_op jit(solution)/shard_map/ppermute | solution.py:12
  611.0 1.2 copy-start.10
  612.9 4.5 copy-start.15
  613.0 4.3 collective-permute-start.1
  632.0 65.2 %all-to-all-start.2 = ((bf16[32,2,1,17920]{3,1,2,0:T(2,128)(2,1)}), bf16[32,2,1,17920]{3,1,2,0:T(2,128)(2,1)S(1)}, u32[]{:S(2)}, u32[]{:S(2)}) async-start(bf16[32,2,1,17920]{3,1,2,0:T(2,128)(2,1)} %copy.34), calls=%async_computation.2 | async-start | bytes 4587520 | tf_op jit(solution)/shard_map/all_to_all | solution.py:30
  638.1 68.4 %collective-permute-start.5 = (bf16[64,3584]{1,0:T(8,128)(2,1)}, bf16[64,3584]{1,0:T(8,128)(2,1)}, u32[]{:S(2)}, u32[]{:S(2)}) collective-permute-start(bf16[64,3584]{1,0:T(8,128)(2,1)} %get-tuple-element.21), channel_id=1, source_target_pairs={{0,448},{64,0},{128,64},{192,128},{256,192},{320,256},{384,320},{4... | collective-permute-start | bytes 1376264 | tf_op jit(solution)/shard_map/ppermute | solution.py:43
  703.4 1.0 copy-start.3
  703.4 1.0 copy-start.13
  704.6 12.6 %collective-permute-start.2 = (bf16[64,3584]{1,0:T(8,128)(2,1)S(1)}, bf16[64,3584]{1,0:T(8,128)(2,1)S(1)}, u32[]{:S(2)}, u32[]{:S(2)}) collective-permute-start(bf16[64,3584]{1,0:T(8,128)(2,1)S(1)} %fusion.8), channel_id=1, source_target_pairs={{0,64},{64,128},{128,192},{192,256},{256,320},{320,384},{384,448},... | collective-permute-start | bytes 1376264 | tf_op jit(solution)/shard_map/ppermute | solution.py:43
where the time goes:
time: 733 us; the launch traced here: 720 us
  waiting for transfers between devices  278 us (38%)
  local copies, waits for them, and re-layouts  170 us (23%)
  blocking collectives  139 us (19%)
  other arithmetic  89.5 us (12%)
  starting transfers between devices  29.8 us (4%)
  matrix products  11 us (2%)
    ppermute x4, waiting for transfers between devices, from_partner(): lax.ppermute(value, axis, [(i, i ^ 1 << stride) for i in range(lax.axis_s...  155 us
    all_to_all x2, blocking collectives, send_rows(): lax.all_to_all(outgoing, EP, split_axis=0, concat_axis=0, tiled=True)  128 us
    all_to_all x2, waiting for transfers between devices, exchange_in_order(): result = lax.all_to_all(result, axes[k], k, k, tiled=True)  113 us
    all_to_all x2, other arithmetic, send_rows(): lax.all_to_all(outgoing, EP, split_axis=0, concat_axis=0, tiled=True)  53.8 us
    slice x1, local copies, waits for them, and re-layouts, member_rows(): arrived.reshape(senders, count, -1)[:, member].reshape(-1, half_width)  52.5 us
    another operation x4, local copies, waits for them, and re-layouts, member_rows(): arrived.reshape(senders, count, -1)[:, member].reshape(-1, half_width)  27.3 us
    unnamed x41, local copies, waits for them, and re-layouts  24.7 us
  transfers between devices with their start and end apart: 8, of which 7 were waited for; matrix products, arithmetic and copies ran while one was open for 1% of the time, Pallas kernels for 0%

commit v1 on v0

v1 whole, which is shorter than its diff:
```python
import functools

import jax
import jax.numpy as jnp
from jax import lax
from jax.experimental import pallas as pl
from jax.experimental.pallas import tpu as pltpu
from jax.sharding import Mesh
from jax.sharding import PartitionSpec as P

EP = ("ep_0", "ep_1", "ep_2")
MESH = pl.DeviceIdType.MESH
BF16, F32 = jnp.bfloat16, jnp.float32
CAP = 10
SLAB = 32
BACK = 16
NT = (((1,), (1,)), ((), ()))


def iota(shape, dim):
    return lax.broadcasted_iota(jnp.int32, shape, dim)


def selector(mask):
    return jnp.where(mask, 1.0, 0.0).astype(BF16)


def dot(a, b):
    return jnp.dot(a, b, preferred_element_type=F32)


def dot_nt(a, b):
    return lax.dot_general(a, b, NT, preferred_element_type=F32)


def aligned(start, size):
    return pl.ds(pl.multiple_of(start, size), size)


def slot_numbers(route):
    count = route.shape[0]
    down, across = iota((count, count), 0), iota((count, count), 1)
    column = route.astype(F32)
    row = jnp.sum(jnp.where(down == across, column, 0.0), axis=0, keepdims=True)
    same = column == row
    row_place = jnp.sum(jnp.where(same & (down < across), 1.0, 0.0), axis=0, keepdims=True)
    column_place = jnp.sum(jnp.where(same & (across < down), 1.0, 0.0), axis=1, keepdims=True)
    return column, column_place, row, row_place


def kernel(
    experts,
    fwd_act,
    fwd_route,
    fwd_gate,
    bwd_act,
    bwd_grad,
    bwd_route,
    bwd_gate,
    gain,
    w_gate,
    w_up,
    w_down,
    fwd_out,
    bwd_out,
    staged,
    outgoing,
    near,
    far,
    rows,
    gate_w,
    up_w,
    down_w,
    pre,
    pre_out,
    pre_in,
    hidden,
    own,
    z_out,
    z_in,
    y_out,
    y_in,
    v_rows,
    results,
    local_sem,
    w_send,
    w_recv,
    a_send,
    a_recv,
    f_send,
    f_recv,
    c_send,
    c_recv,
    z_send,
    z_recv,
    y_send,
    y_recv,
    p_send,
    p_recv,
):
    tokens, width = fwd_act.shape
    half = width // 2
    tile = min(256, half)
    tiles = half // tile
    slabs = 2 * experts
    block = slabs * CAP
    section, y, z, c = (lax.axis_index(a) for a in ("pp", *EP))
    sections = lax.axis_size("pp")
    me = y * 2 + c
    core = 1 - c
    z_weights = z + 1 - 2 * lax.rem(z, 2)
    z_rows = lax.rem(z + 2 * lax.rem(z, 2) + 3, 4)
    following = lax.rem(section + 1, sections)
    previous = lax.rem(section + sections - 1, sections)

    def y_at(step, sign):
        away = (step + 1) // 2 * (2 * lax.rem(step, 2) - 1)
        return lax.rem(y + sign * away + 2 * experts, experts)

    def send(src, dst, sems, index, recv_sems, recv_index, device):
        return pltpu.make_async_remote_copy(
            src_ref=src,
            dst_ref=dst,
            send_sem=sems.at[index],
            recv_sem=recv_sems.at[recv_index],
            device_id=device,
            device_id_type=MESH,
        )

    barrier = pltpu.get_barrier_semaphore()

    def greet(device):
        pl.semaphore_signal(barrier, inc=1, device_id=device, device_id_type=MESH)

    def greet_row(step, _):
        there = y_at(step, 1)
        greet((section, there, z, 0))
        greet((section, there, z, 1))
        return 0

    greet((section, y, z_weights, c))
    greet((section, y, z_rows, c))
    greet((following, y, z, c))
    greet((previous, y, z, c))
    greet((section, y, z, core))
    lax.fori_loop(1, experts, greet_row, 0)

    weights = ((w_gate, gate_w), (w_up, up_w), (w_down, down_w))
    kept = [
        pltpu.make_async_copy(src, dst.at[0], local_sem.at[i])
        for i, (src, dst) in enumerate(weights)
    ]
    for copy in kept:
        copy.start()

    pl.semaphore_wait(barrier, 2 * experts + 3)

    swapped = [
        send(src, dst.at[1], w_send, i, w_recv, i, (section, y, z_weights, c))
        for i, (src, dst) in enumerate(weights)
    ]
    for copy in swapped:
        copy.start()

    def normalized(ref, slot):
        wide = ref[...].astype(F32)
        inverse = lax.rsqrt(jnp.mean(wide * wide, axis=-1, keepdims=True) + 1e-06)
        staged[slot] = (wide * inverse * gain[...]).astype(BF16)
        return inverse

    normalized(fwd_act, 0)
    bwd_inverse = normalized(bwd_act, 1)
    staged[2] = (bwd_gate[...] * bwd_grad[...].astype(F32)).astype(BF16)

    fwd_slots = slot_numbers(fwd_route[...])
    bwd_slots = slot_numbers(bwd_route[...])

    def placing(slots, offset):
        target = (slots[2] * SLAB + slots[3]).astype(jnp.int32) + offset
        return selector(iota((experts * SLAB, tokens), 0) == target)

    place_fwd = placing(fwd_slots, 0)
    place_bwd = placing(bwd_slots, CAP)
    place_grad = placing(bwd_slots, 2 * CAP)

    def place_half(k, _):
        def place_tile(i, _):
            source = aligned(k * half + i * tile, tile)
            placed = dot(place_fwd, staged[0, :, source])
            placed += dot(place_bwd, staged[1, :, source])
            placed += dot(place_grad, staged[2, :, source])
            outgoing[k, :, aligned(i * tile, tile)] = placed.astype(BF16)
            return 0

        return lax.fori_loop(0, tiles, place_tile, 0)

    lax.fori_loop(0, 2, place_half, 0)

    def slab(index):
        return aligned(index * SLAB, SLAB)

    def dispatch(step, k):
        there = y_at(step, 1)
        return send(
            outgoing.at[k, slab(there)],
            near.at[slab(me)],
            a_send,
            step * 2 + k,
            a_recv,
            me,
            (section, there, z, k),
        )

    def dispatch_row(step, _):
        dispatch(step, 0).start()
        dispatch(step, 1).start()
        return 0

    stay = pltpu.make_async_copy(outgoing.at[c, slab(y)], near.at[slab(me)], local_sem.at[3])
    stay.start()
    dispatch(0, core).start()
    lax.fori_loop(1, experts, dispatch_row, 0)

    def arrival(index):
        return send(
            outgoing.at[0, slab(0)],
            near.at[slab(index)],
            a_send,
            0,
            a_recv,
            index,
            (section, y, z, core),
        )

    def forward(index):
        return send(
            near.at[slab(index)],
            far.at[slab(index)],
            f_send,
            index,
            f_recv,
            index,
            (section, y, z_rows, c),
        )

    def forward_row(step, _):
        there = y_at(step, -1) * 2
        for from_core in range(2):
            arrival(there + from_core).wait_recv()
            forward(there + from_core).start()
        return 0

    stay.wait()
    forward(me).start()
    arrival(y * 2 + core).wait_recv()
    forward(y * 2 + core).start()
    lax.fori_loop(1, experts, forward_row, 0)

    source = iota((3 * block, slabs * SLAB), 1)
    within = source & (SLAB - 1)
    kind = (within >= CAP).astype(jnp.int32) + (within >= 2 * CAP).astype(jnp.int32)
    target = kind * block + (source // SLAB) * CAP + within - kind * CAP
    dense = selector(
        (iota((3 * block, slabs * SLAB), 0) == target) & (within < 3 * CAP)
    )

    def take_apart(slab_rows, first):
        def apart(i, _):
            columns = aligned(i * tile, tile)
            values = dot(dense, slab_rows[:, columns]).astype(BF16)
            for kind in range(3):
                rows[kind, first : first + block, columns] = values[
                    kind * block : (kind + 1) * block
                ]
            return 0

        lax.fori_loop(0, tiles, apart, 0)

    take_apart(near, 0)

    def far_arrived(index, _):
        forward(index).wait_recv()
        return 0

    lax.fori_loop(0, slabs, far_arrived, 0)
    take_apart(far, block)

    def first_products(b):
        def of_rows(kind, _):
            for which, weight in ((0, gate_w), (1, up_w)):
                product = dot(rows[kind], weight[b])
                pre[b, 2 * kind + which] = product
                pre_out[b, 2 * kind + which] = product.astype(BF16)
            return 0

        lax.fori_loop(0, 2, of_rows, 0)

    def down_product(b):
        product = dot_nt(rows[2], down_w[b])
        pre[b, 4] = product
        pre_out[b, 4] = product.astype(BF16)

    def cross(b, first, count, index):
        part = pl.ds(first, count)
        return send(
            pre_out.at[b, part],
            pre_in.at[b, part],
            c_send,
            index,
            c_recv,
            index,
            (section, y, z, core),
        )

    def activate(b):
        gate_pre = pre[b, 0] + pre_in[b, 0].astype(F32)
        up_pre = pre[b, 1] + pre_in[b, 1].astype(F32)
        hidden[b, 0] = (gate_pre * jax.nn.sigmoid(gate_pre) * up_pre).astype(BF16)

    def derive(b):
        gate_pre = pre[b, 2] + pre_in[b, 2].astype(F32)
        up_pre = pre[b, 3] + pre_in[b, 3].astype(F32)
        grad = pre[b, 4] + pre_in[b, 4].astype(F32)
        logistic = jax.nn.sigmoid(gate_pre)
        hidden[b, 1] = (
            grad * up_pre * logistic * (1.0 + gate_pre * (1.0 - logistic))
        ).astype(BF16)
        hidden[b, 2] = (grad * gate_pre * logistic).astype(BF16)

    for copy in kept:
        copy.wait()
    first_products(0)
    down_product(0)
    cross(0, 0, 5, 0).start()

    swapped[0].wait_recv()
    swapped[1].wait_recv()
    first_products(1)
    cross(1, 0, 4, 1).start()
    cross(0, 0, 5, 0).wait_recv()
    activate(0)
    derive(0)
    cross(1, 0, 4, 1).wait_recv()
    activate(1)

    swapped[2].wait_recv()
    down_product(1)
    cross(1, 4, 1, 2).start()

    def give_back(which):
        return send(
            z_out.at[which], z_in.at[which], z_send, which, z_recv, which, (section, y, z_rows, c)
        )

    def split(which, columns, values):
        own[which, :, columns] = values[:block]
        z_out[which, :, columns] = values[block:].astype(BF16)

    def forward_tile(i, _):
        columns = aligned(i * tile, tile)
        split(
            0,
            columns,
            dot(hidden[0, 0], down_w[0, :, columns]) + dot(hidden[1, 0], down_w[1, :, columns]),
        )
        return 0

    lax.fori_loop(0, tiles, forward_tile, 0)
    give_back(0).start()

    cross(1, 4, 1, 2).wait_recv()
    derive(1)

    def backward_tile(i, _):
        columns = aligned(i * tile, tile)
        values = dot_nt(hidden[0, 1], gate_w[0, columns, :])
        values += dot_nt(hidden[1, 1], gate_w[1, columns, :])
        values += dot_nt(hidden[0, 2], up_w[0, columns, :])
        values += dot_nt(hidden[1, 2], up_w[1, columns, :])
        split(1, columns, values)
        return 0

    lax.fori_loop(0, tiles, backward_tile, 0)
    give_back(1).start()

    back = iota((slabs * BACK, block), 0)
    place = back & (BACK - 1)
    spread = selector(
        (iota((slabs * BACK, block), 1) == (back // BACK) * CAP + place) & (place < CAP)
    )

    def slots_of(index):
        return aligned(index * BACK, BACK)

    def returning(which, step, to_core):
        there = y_at(step, 1)
        return send(
            y_out.at[which, slots_of(there * 2 + to_core)],
            y_in.at[which, c, slots_of(y)],
            y_send.at[which],
            step * 2 + to_core,
            y_recv.at[which],
            y * 2 + c,
            (section, there, z, to_core),
        )

    def staying(which):
        return pltpu.make_async_copy(
            y_out.at[which, slots_of(me)],
            y_in.at[which, c, slots_of(y)],
            local_sem.at[4 + which],
        )

    def send_back(which):
        give_back(which).wait_recv()

        def spread_tile(i, _):
            columns = aligned(i * tile, tile)
            total = (own[which, :, columns] + z_in[which, :, columns].astype(F32)).astype(BF16)
            y_out[which, :, columns] = dot(spread, total).astype(BF16)
            return 0

        lax.fori_loop(0, tiles, spread_tile, 0)

        def return_row(step, _):
            returning(which, step, 0).start()
            returning(which, step, 1).start()
            return 0

        staying(which).start()
        returning(which, 0, core).start()
        lax.fori_loop(1, experts, return_row, 0)

    def returned(which, index, k, e):
        return send(
            y_out.at[which, slots_of(0)],
            y_in.at[which, k, slots_of(e)],
            y_send.at[which],
            0,
            y_recv.at[which],
            index,
            (section, y, z, core),
        )

    def collect(which):
        def from_row(step, _):
            there = y_at(step, -1)
            returned(which, there * 2, 0, there).wait_recv()
            returned(which, there * 2 + 1, 1, there).wait_recv()
            return 0

        staying(which).wait()
        returned(which, y * 2 + core, core, y).wait_recv()
        lax.fori_loop(1, experts, from_row, 0)

    send_back(0)
    send_back(1)

    def picking(slots):
        target = (slots[0] * BACK + slots[1]).astype(jnp.int32)
        return selector(iota((tokens, experts * BACK), 1) == target)

    collect(0)
    pick_fwd = picking(fwd_slots)

    def forward_half(k, _):
        def finish(i, _):
            columns = aligned(k * half + i * tile, tile)
            mixed = dot(pick_fwd, y_in[0, k, :, aligned(i * tile, tile)])
            results[0, :, columns] = (
                fwd_act[:, columns].astype(F32) + fwd_gate[...] * mixed
            ).astype(BF16)
            return 0

        return lax.fori_loop(0, tiles, finish, 0)

    lax.fori_loop(0, 2, forward_half, 0)
    to_next = send(results.at[0], fwd_out, p_send, 0, p_recv, 0, (following, y, z, c))
    to_next.start()

    collect(1)
    pick_bwd = picking(bwd_slots)

    def gather_half(k, dotted):
        def gather(i, dotted):
            columns = aligned(k * half + i * tile, tile)
            scaled = gain[:, columns] * dot(pick_bwd, y_in[1, k, :, aligned(i * tile, tile)])
            v_rows[:, columns] = scaled
            return dotted + scaled * bwd_act[:, columns].astype(F32)

        return lax.fori_loop(0, tiles, gather, dotted)

    dotted = lax.fori_loop(0, 2, gather_half, jnp.zeros((tokens, tile), F32))
    mean = jnp.sum(dotted, axis=-1, keepdims=True) / width
    factor = bwd_inverse * bwd_inverse * bwd_inverse * mean

    def backward_finish(i, _):
        columns = aligned(i * tile, tile)
        results[1, :, columns] = (
            bwd_grad[:, columns].astype(F32)
            + v_rows[:, columns] * bwd_inverse
            - bwd_act[:, columns].astype(F32) * factor
        ).astype(BF16)
        return 0

    lax.fori_loop(0, 2 * tiles, backward_finish, 0)
    to_previous = send(results.at[1], bwd_out, p_send, 1, p_recv, 1, (previous, y, z, c))
    to_previous.start()

    for copy in swapped:
        copy.wait_send()
    dispatch(0, core).wait_send()
    returning(0, 0, core).wait_send()
    returning(1, 0, core).wait_send()

    def row_left(step, _):
        for k in range(2):
            dispatch(step, k).wait_send()
            returning(0, step, k).wait_send()
            returning(1, step, k).wait_send()
        return 0

    lax.fori_loop(1, experts, row_left, 0)

    def forward_left(index, _):
        forward(index).wait_send()
        return 0

    lax.fori_loop(0, slabs, forward_left, 0)
    cross(0, 0, 5, 0).wait_send()
    cross(1, 0, 4, 1).wait_send()
    cross(1, 4, 1, 2).wait_send()
    give_back(0).wait_send()
    give_back(1).wait_send()
    to_next.wait()
    to_previous.wait()


def body(
    fwd_act,
    fwd_route,
    fwd_gate,
    bwd_act,
    bwd_grad,
    bwd_route,
    bwd_gate,
    norm_gain,
    w_gate,
    w_up,
    w_down,
):
    experts = lax.axis_size("ep_0")
    _, tokens, width = fwd_act.shape
    _, _, half, units = w_gate.shape
    slabs = 2 * experts
    block = slabs * CAP
    dma = pltpu.SemaphoreType.DMA
    vmem = pl.BlockSpec(memory_space=pltpu.VMEM)
    anywhere = pl.BlockSpec(memory_space=pl.ANY)
    outs = pl.pallas_call(
        functools.partial(kernel, experts),
        out_shape=[jax.ShapeDtypeStruct((tokens, width), BF16)] * 2,
        in_specs=[vmem] * 8 + [anywhere] * 3,
        out_specs=[vmem] * 2,
        scratch_shapes=[
            pltpu.VMEM((3, tokens, width), BF16),
            pltpu.VMEM((2, experts * SLAB, half), BF16),
            pltpu.VMEM((slabs * SLAB, half), BF16),
            pltpu.VMEM((slabs * SLAB, half), BF16),
            pltpu.VMEM((3, 2 * block, half), BF16),
            pltpu.VMEM((2, half, units), BF16),
            pltpu.VMEM((2, half, units), BF16),
            pltpu.VMEM((2, units, half), BF16),
            pltpu.VMEM((2, 5, 2 * block, units), F32),
            pltpu.VMEM((2, 5, 2 * block, units), BF16),
            pltpu.VMEM((2, 5, 2 * block, units), BF16),
            pltpu.VMEM((2, 3, 2 * block, units), BF16),
            pltpu.VMEM((2, block, half), F32),
            pltpu.VMEM((2, block, half), BF16),
            pltpu.VMEM((2, block, half), BF16),
            pltpu.VMEM((2, slabs * BACK, half), BF16),
            pltpu.VMEM((2, 2, experts * BACK, half), BF16),
            pltpu.VMEM((tokens, width), F32),
            pltpu.VMEM((2, tokens, width), BF16),
            dma((6,)),
            dma((3,)),
            dma((3,)),
            dma((slabs,)),
            dma((slabs,)),
            dma((slabs,)),
            dma((slabs,)),
            dma((3,)),
            dma((3,)),
            dma((2,)),
            dma((2,)),
            dma((2, slabs)),
            dma((2, slabs)),
            dma((2,)),
            dma((2,)),
        ],
        compiler_params=pltpu.CompilerParams(
            collective_id=0, has_side_effects=True, vmem_limit_bytes=60 * 1024 * 1024
        ),
        name="relay_layer",
    )(
        fwd_act[0],
        fwd_route[0],
        fwd_gate[0],
        bwd_act[0],
        bwd_grad[0],
        bwd_route[0],
        bwd_gate[0],
        norm_gain,
        w_gate[0, 0],
        w_up[0, 0],
        w_down[0, 0],
    )
    return tuple(out[None] for out in outs)


def solution(mesh):
    sections = mesh.shape["pp"]
    split = Mesh(
        mesh.devices.reshape(sections, mesh.shape["ep"] // 8, 4, 2), ("pp", "ep_0", "ep_1", "ep_2")
    )
    rows = P("pp", EP, None)
    weights = P("pp", EP, None, None)
    return jax.shard_map(
        body,
        mesh=split,
        in_specs=(rows,) * 7 + (P("pp", None),) + (weights,) * 3,
        out_specs=(rows, rows),
        check_vma=False,
    )
```

time: 733 us -> 240 us (0.33); the launches traced: 720 us -> 240 us
  waiting for transfers between devices: 278 us -> 0 us
  Pallas kernels: 0 us -> 233 us
  local copies, waits for them, and re-layouts: 170 us -> 6.11 us
  blocking collectives: 139 us -> 0 us
  other arithmetic: 89.5 us -> 0 us
  starting transfers between devices: 29.8 us -> 0 us
  matrix products: 11 us -> 0 us
    pallas_call x0 -> x1, Pallas kernels: none -> 233 us  [body(): pl.pallas_call(functools.partial(kernel, experts), out_shape=[jax.ShapeDt...]
    ppermute x6 -> x0, waiting for transfers between devices: 165 us -> none  [the longest x4 155 us: from_partner(): lax.ppermute(value, axis, [(i, i ^ 1 << stride) for i in range(lax.axis_s...]
    all_to_all x4 -> x0, blocking collectives: 139 us -> none  [the longest x2 128 us: send_rows(): lax.all_to_all(outgoing, EP, split_axis=0, concat_axis=0, tiled=True)]
    all_to_all x2 -> x0, waiting for transfers between devices: 113 us -> none  [exchange_in_order(): result = lax.all_to_all(result, axes[k], k, k, tiled=True)]
    slice x7 -> x0, local copies, waits for them, and re-layouts: 59.9 us -> none  [the longest x1 52.5 us: member_rows(): arrived.reshape(senders, count, -1)[:, member].reshape(-1, half_width)]
    all_to_all x2 -> x0, other arithmetic: 53.8 us -> none  [send_rows(): lax.all_to_all(outgoing, EP, split_axis=0, concat_axis=0, tiled=True)]
    another operation x26 -> x0, local copies, waits for them, and re-layouts: 45.3 us -> none  [the longest x4 27.3 us: member_rows(): arrived.reshape(senders, count, -1)[:, member].reshape(-1, half_width)]
    unnamed x41 -> x12, local copies, waits for them, and re-layouts: 24.7 us -> 3.3 us
  transfers between devices with their start and end apart: 8 -> 0, of which waited for: 7 -> 0; matrix products, arithmetic and copies ran while one was open for 1% -> 0% of each run, Pallas kernels for 0% -> 0%
where the time goes in v1:
time: 240 us
  Pallas kernels  233 us (97%)
  local copies, waits for them, and re-layouts  6.11 us (3%)
    pallas_call x1, Pallas kernels, body(): pl.pallas_call(functools.partial(kernel, experts), out_shape=[jax.ShapeDt...  233 us

profile of v1, /device:TPU:1, one launch (start us, length us, event | category | flops | bytes accessed | tf_op | source)
XLA Modules:
  0.0 240.1 jit_solution(1049377509331569689)
XLA Ops:
  0.6 0.0 copy-start.1
  0.6 0.6 copy-done.1
  1.3 0.0 copy-start.2
  1.3 0.7 copy.13.fwd_route
  2.0 0.0 copy-done.2
  2.0 0.0 copy-start.3
  2.0 0.7 copy.14.fwd_gate
  2.7 0.0 copy-done.3
  2.7 0.0 copy-start.4
  2.7 0.7 copy.15.bwd_route
  3.4 0.0 copy-done.4
  3.4 0.7 copy.16.bwd_gate
  4.1 233.3 %relay_layer.1 = (bf16[64,3584]{1,0:T(8,128)(2,1)}, bf16[64,3584]{1,0:T(8,128)(2,1)}) custom-call(bf16[64,3584]{1,0:T(8,128)(2,1)} %bitcast.15, s32[64,1]{1,0:T(8,128)} %copy.13.fwd_route, f32[64,1]{1,0:T(8,128)} %copy.14.fwd_gate, bf16[64,3584]{1,0:T(8,128)(2,1)} %bitcast.16, bf16[64,3584]{1,0:T(8,128)(2,1)} %bitcast.17, s32[64,1]{1,0:T(8,128)} %copy.15.bwd_route, ...), custom_call_target="tpu_custom_call" | custom-call | tf_op jit(solution)/shard_map/relay_layer/pallas_call | solution.py:560
  237.4 0.0 copy-start
  237.4 1.9 copy.19
  239.3 0.0 copy-done
  239.3 0.8 copy.20
Async XLA Ops:
  0.6 0.7 copy-start.1
  1.3 0.7 copy-start.2
  2.0 0.7 copy-start.3
  2.7 0.7 copy-start.4
  237.4 1.9 copy-start

commit v2 on v1

--- a/solution.py
+++ b/solution.py
@@ -15,6 +15,8 @@
 SLAB = 32
 BACK = 16
 NT = (((1,), (1,)), ((), ()))
+PIECES = ((0, 2), (2, 3), (5, 2))
+DETOUR = 80
 
 
 def iota(shape, dim):
@@ -37,11 +39,17 @@
     return pl.ds(pl.multiple_of(start, size), size)
 
 
+def as_column(row):
+    count = row.shape[1]
+    mine = iota((count, count), 0) == iota((count, count), 1)
+    return jnp.sum(jnp.where(mine, row, 0.0), axis=1, keepdims=True)
+
+
 def slot_numbers(route):
-    count = route.shape[0]
+    count = route.shape[1]
     down, across = iota((count, count), 0), iota((count, count), 1)
-    column = route.astype(F32)
-    row = jnp.sum(jnp.where(down == across, column, 0.0), axis=0, keepdims=True)
+    row = route.astype(F32)
+    column = as_column(row)
     same = column == row
     row_place = jnp.sum(jnp.where(same & (down < across), 1.0, 0.0), axis=0, keepdims=True)
     column_place = jnp.sum(jnp.where(same & (across < down), 1.0, 0.0), axis=1, keepdims=True)
@@ -82,6 +90,8 @@
     y_in,
     v_rows,
     results,
+    passing_w,
+    passing_z,
     local_sem,
     w_send,
     w_recv,
@@ -97,6 +107,8 @@
     y_recv,
     p_send,
     p_recv,
+    d_send,
+    d_recv,
 ):
     tokens, width = fwd_act.shape
     half = width // 2
@@ -108,8 +120,11 @@
     sections = lax.axis_size("pp")
     me = y * 2 + c
     core = 1 - c
-    z_weights = z + 1 - 2 * lax.rem(z, 2)
-    z_rows = lax.rem(z + 2 * lax.rem(z, 2) + 3, 4)
+    odd_column = lax.rem(section // 2, 2)
+    turn = 2 * lax.rem(z + odd_column, 2)
+    z_weights = lax.rem(z + 5 - turn, 4)
+    z_rows = lax.rem(z + 3 + turn, 4)
+    beside = section + 2 - 4 * odd_column
     following = lax.rem(section + 1, sections)
     previous = lax.rem(section + sections - 1, sections)
 
@@ -140,6 +155,7 @@
 
     greet((section, y, z_weights, c))
     greet((section, y, z_rows, c))
+    greet((beside, y, z, c))
     greet((following, y, z, c))
     greet((previous, y, z, c))
     greet((section, y, z, core))
@@ -153,11 +169,51 @@
     for copy in kept:
         copy.start()
 
-    pl.semaphore_wait(barrier, 2 * experts + 3)
-
+    pl.semaphore_wait(barrier, 2 * experts + 4)
+
+    units = w_down.shape[0] - DETOUR
+    pieces = PIECES
+
+    def piece_columns(piece):
+        start, count = pieces[piece]
+        return pl.ds(start * tile, count * tile)
+
+    def detour(which, step):
+        if which == 2:
+            stops = (
+                w_down.at[pl.ds(units, DETOUR)],
+                passing_w.at[0],
+                passing_w.at[1],
+                down_w.at[1, pl.ds(units, DETOUR)],
+            )
+        else:
+            columns = piece_columns(0)
+            stops = (
+                z_out.at[which, :, columns],
+                passing_z.at[0, which],
+                passing_z.at[1, which],
+                z_in.at[which, :, columns],
+            )
+        along_z = (section, y, z_rows if which == 2 else z_weights, c)
+        return send(
+            stops[step],
+            stops[step + 1],
+            d_send,
+            which * 3 + step,
+            d_recv,
+            which * 3 + step,
+            along_z if step == 1 else (beside, y, z, c),
+        )
+
+    detour(2, 0).start()
+    swaps = (
+        (w_gate, gate_w.at[1]),
+        (w_up, up_w.at[1]),
+        (w_down.at[pl.ds(0, units)], down_w.at[1, pl.ds(0, units)]),
+    )
     swapped = [
-        send(src, dst.at[1], w_send, i, w_recv, i, (section, y, z_weights, c))
-        for i, (src, dst) in enumerate(weights)
+        send(src, dst, w_send, i, w_recv, i, (section, y, z_weights, c))
+        for i, (src, dst) in enumerate(swaps)
     ]
     for copy in swapped:
         copy.start()
@@ -170,7 +226,7 @@
 
     normalized(fwd_act, 0)
     bwd_inverse = normalized(bwd_act, 1)
-    staged[2] = (bwd_gate[...] * bwd_grad[...].astype(F32)).astype(BF16)
+    staged[2] = (as_column(bwd_gate[...]) * bwd_grad[...].astype(F32)).astype(BF16)
 
     fwd_slots = slot_numbers(fwd_route[...])
     bwd_slots = slot_numbers(bwd_route[...])
@@ -220,6 +276,8 @@
     stay.start()
     dispatch(0, core).start()
     lax.fori_loop(1, experts, dispatch_row, 0)
+    detour(2, 0).wait_recv()
+    detour(2, 1).start()
 
     def arrival(index):
         return send(
@@ -277,6 +335,8 @@
         lax.fori_loop(0, tiles, apart, 0)
 
     take_apart(near, 0)
+    detour(2, 1).wait_recv()
+    detour(2, 2).start()
 
     def far_arrived(index, _):
         forward(index).wait_recv()
@@ -344,13 +404,29 @@
     activate(1)
 
     swapped[2].wait_recv()
+    detour(2, 2).wait_recv()
     down_product(1)
     cross(1, 4, 1, 2).start()
 
-    def give_back(which):
+    def give_back(which, piece):
+        columns = piece_columns(piece)
         return send(
-            z_out.at[which], z_in.at[which], z_send, which, z_recv, which, (section, y, z_rows, c)
-        )
+            z_out.at[which, :, columns],
+            z_in.at[which, :, columns],
+            z_send.at[which],
+            piece,
+            z_recv.at[which],
+            piece,
+            (section, y, z_rows, c),
+        )
+
+    def give_back_all(which, one_tile):
+        for piece, (start, count) in enumerate(pieces):
+            lax.fori_loop(start, start + count, one_tile, 0)
+            if piece == 0:
+                detour(which, 0).start()
+            else:
+                give_back(which, piece).start()
 
     def split(which, columns, values):
         own[which, :, columns] = values[:block]
@@ -365,8 +441,7 @@
         )
         return 0
 
-    lax.fori_loop(0, tiles, forward_tile, 0)
-    give_back(0).start()
+    give_back_all(0, forward_tile)
 
     cross(1, 4, 1, 2).wait_recv()
     derive(1)
@@ -380,8 +455,7 @@
         split(1, columns, values)
         return 0
 
-    lax.fori_loop(0, tiles, backward_tile, 0)
-    give_back(1).start()
+    give_back_all(1, backward_tile)
 
     back = iota((slabs * BACK, block), 0)
     place = back & (BACK - 1)
@@ -392,27 +466,33 @@
     def slots_of(index):
         return aligned(index * BACK, BACK)
 
-    def returning(which, step, to_core):
+    def returning(which, piece, step, to_core):
         there = y_at(step, 1)
+        columns = piece_columns(piece)
         return send(
-            y_out.at[which, slots_of(there * 2 + to_core)],
-            y_in.at[which, c, slots_of(y)],
-            y_send.at[which],
+            y_out.at[which, slots_of(there * 2 + to_core), columns],
+            y_in.at[which, c, slots_of(y), columns],
+            y_send.at[which, piece],
             step * 2 + to_core,
-            y_recv.at[which],
+            y_recv.at[which, piece],
             y * 2 + c,
             (section, there, z, to_core),
         )
 
-    def staying(which):
+    def staying(which, piece):
+        columns = piece_columns(piece)
         return pltpu.make_async_copy(
-            y_out.at[which, slots_of(me)],
-            y_in.at[which, c, slots_of(y)],
-            local_sem.at[4 + which],
-        )
-
-    def send_back(which):
-        give_back(which).wait_recv()
+            y_out.at[which, slots_of(me), columns],
+            y_in.at[which, c, slots_of(y), columns],
+            local_sem.at[4 + which * len(PIECES) + piece],
+        )
+
+    def send_back(which, piece):
+        if piece == 0:
+            detour(which, 2).wait_recv()
+        else:
+            give_back(which, piece).wait_recv()
+        first, count = pieces[piece]
 
         def spread_tile(i, _):
             columns = aligned(i * tile, tile)
@@ -420,77 +500,90 @@
             y_out[which, :, columns] = dot(spread, total).astype(BF16)
             return 0
 
-        lax.fori_loop(0, tiles, spread_tile, 0)
+        lax.fori_loop(first, first + count, spread_tile, 0)
 
         def return_row(step, _):
-            returning(which, step, 0).start()
-            returning(which, step, 1).start()
+            returning(which, piece, step, 0).start()
+            returning(which, piece, step, 1).start()
             return 0
 
-        staying(which).start()
-        returning(which, 0, core).start()
+        staying(which, piece).start()
+        returning(which, piece, 0, core).start()
         lax.fori_loop(1, experts, return_row, 0)
 
-    def returned(which, index, k, e):
+    def returned(which, piece, k, e):
+        columns = piece_columns(piece)
         return send(
-            y_out.at[which, slots_of(0)],
-            y_in.at[which, k, slots_of(e)],
-            y_send.at[which],
+            y_out.at[which, slots_of(0), columns],
+            y_in.at[which, k, slots_of(e), columns],
+            y_send.at[which, piece],
             0,
-            y_recv.at[which],
-            index,
+            y_recv.at[which, piece],
+            e * 2 + k,
             (section, y, z, core),
         )
 
-    def collect(which):
+    def collect(which, piece):
         def from_row(step, _):
             there = y_at(step, -1)
-            returned(which, there * 2, 0, there).wait_recv()
-            returned(which, there * 2 + 1, 1, there).wait_recv()
+            returned(which, piece, 0, there).wait_recv()
+            returned(which, piece, 1, there).wait_recv()
             return 0
 
-        staying(which).wait()
-        returned(which, y * 2 + core, core, y).wait_recv()
+        staying(which, piece).wait()
+        returned(which, piece, core, y).wait_recv()
         lax.fori_loop(1, experts, from_row, 0)
 
-    send_back(0)
-    send_back(1)
+    detour(0, 0).wait_recv()
+    detour(0, 1).start()
+    detour(1, 0).wait_recv()
+    detour(1, 1).start()
+    send_back(0, 1)
+    detour(0, 1).wait_recv()
+    detour(0, 2).start()
+    send_back(0, 2)
+    send_back(0, 0)
+    detour(1, 1).wait_recv()
+    detour(1, 2).start()
+    for piece in range(len(pieces)):
+        send_back(1, piece)
 
     def picking(slots):
         target = (slots[0] * BACK + slots[1]).astype(jnp.int32)
         return selector(iota((tokens, experts * BACK), 1) == target)
 
-    collect(0)
     pick_fwd = picking(fwd_slots)
-
-    def forward_half(k, _):
-        def finish(i, _):
-            columns = aligned(k * half + i * tile, tile)
-            mixed = dot(pick_fwd, y_in[0, k, :, aligned(i * tile, tile)])
-            results[0, :, columns] = (
-                fwd_act[:, columns].astype(F32) + fwd_gate[...] * mixed
-            ).astype(BF16)
-            return 0
-
-        return lax.fori_loop(0, tiles, finish, 0)
-
-    lax.fori_loop(0, 2, forward_half, 0)
+    fwd_scale = as_column(fwd_gate[...])
+    for piece in (1, 2, 0):
+        start, count = pieces[piece]
+        collect(0, piece)
+        for k in range(2):
+
+            def finish(i, _):
+                columns = aligned(k * half + i * tile, tile)
+                mixed = dot(pick_fwd, y_in[0, k, :, aligned(i * tile, tile)])
+                results[0, :, columns] = (
+                    fwd_act[:, columns].astype(F32) + fwd_scale * mixed
+                ).astype(BF16)
+                return 0
+
+            lax.fori_loop(start, start + count, finish, 0)
     to_next = send(results.at[0], fwd_out, p_send, 0, p_recv, 0, (following, y, z, c))
     to_next.start()
 
-    collect(1)
     pick_bwd = picking(bwd_slots)
-
-    def gather_half(k, dotted):
-        def gather(i, dotted):
-            columns = aligned(k * half + i * tile, tile)
-            scaled = gain[:, columns] * dot(pick_bwd, y_in[1, k, :, aligned(i * tile, tile)])
-            v_rows[:, columns] = scaled
-            return dotted + scaled * bwd_act[:, columns].astype(F32)
-
-        return lax.fori_loop(0, tiles, gather, dotted)
-
-    dotted = lax.fori_loop(0, 2, gather_half, jnp.zeros((tokens, tile), F32))
+    dotted = jnp.zeros((tokens, tile), F32)
+    for piece, (start, count) in enumerate(pieces):
+        collect(1, piece)
+        for k in range(2):
+
+            def gather(i, dotted):
+                columns = aligned(k * half + i * tile, tile)
+                scaled = gain[:, columns] * dot(pick_bwd, y_in[1, k, :, aligned(i * tile, tile)])
+                v_rows[:, columns] = scaled
+                return dotted + scaled * bwd_act[:, columns].astype(F32)
+
+            dotted = lax.fori_loop(start, start + count, gather, dotted)
     mean = jnp.sum(dotted, axis=-1, keepdims=True) / width
     factor = bwd_inverse * bwd_inverse * bwd_inverse * mean
 
@@ -509,15 +602,22 @@
 
     for copy in swapped:
         copy.wait_send()
+    for which in range(3):
+        for step in range(3):
+            detour(which, step).wait_send()
     dispatch(0, core).wait_send()
-    returning(0, 0, core).wait_send()
-    returning(1, 0, core).wait_send()
+    for which in range(2):
+        for piece in range(len(pieces)):
+            returning(which, piece, 0, core).wait_send()
+            if piece:
+                give_back(which, piece).wait_send()
 
     def row_left(step, _):
         for k in range(2):
             dispatch(step, k).wait_send()
-            returning(0, step, k).wait_send()
-            returning(1, step, k).wait_send()
+            for which in range(2):
+                for piece in range(len(pieces)):
+                    returning(which, piece, step, k).wait_send()
         return 0
 
     lax.fori_loop(1, experts, row_left, 0)
@@ -530,8 +630,6 @@
     cross(0, 0, 5, 0).wait_send()
     cross(1, 0, 4, 1).wait_send()
     cross(1, 4, 1, 2).wait_send()
-    give_back(0).wait_send()
-    give_back(1).wait_send()
     to_next.wait()
     to_previous.wait()
 
@@ -582,7 +680,9 @@
             pltpu.VMEM((2, 2, experts * BACK, half), BF16),
             pltpu.VMEM((tokens, width), F32),
             pltpu.VMEM((2, tokens, width), BF16),
-            dma((6,)),
+            pltpu.VMEM((2, DETOUR, half), BF16),
+            pltpu.VMEM((2, 2, block, PIECES[0][1] * 256), BF16),
+            dma((4 + 2 * len(PIECES),)),
             dma((3,)),
             dma((3,)),
             dma((slabs,)),
@@ -591,12 +691,14 @@
             dma((slabs,)),
             dma((3,)),
             dma((3,)),
+            dma((2, len(PIECES))),
+            dma((2, len(PIECES))),
+            dma((2, len(PIECES), slabs)),
+            dma((2, len(PIECES), slabs)),
             dma((2,)),
             dma((2,)),
-            dma((2, slabs)),
-            dma((2, slabs)),
-            dma((2,)),
-            dma((2,)),
+            dma((9,)),
+            dma((9,)),
         ],
         compiler_params=pltpu.CompilerParams(
             collective_id=0, has_side_effects=True, vmem_limit_bytes=60 * 1024 * 1024
@@ -604,12 +706,12 @@
         name="relay_layer",
     )(
         fwd_act[0],
-        fwd_route[0],
-        fwd_gate[0],
+        fwd_route[:, :, 0],
+        fwd_gate[:, :, 0],
         bwd_act[0],
         bwd_grad[0],
-        bwd_route[0],
-        bwd_gate[0],
+        bwd_route[:, :, 0],
+        bwd_gate[:, :, 0],
         norm_gain,
         w_gate[0, 0],
         w_up[0, 0],

time: 240 us -> 207 us (0.86)
  Pallas kernels: 233 us -> 204 us
  local copies, waits for them, and re-layouts: 6.11 us -> 2.64 us
    pallas_call x1, Pallas kernels: 233 us -> 204 us  [body(): pl.pallas_call(functools.partial(kernel, experts), out_shape=[jax.ShapeDt...]
    squeeze x4 -> x0, local copies, waits for them, and re-layouts: 2.81 us -> none  [the longest x1 0.71 us: body(): fwd_gate[0]]
where the time goes in v2:
time: 207 us
  Pallas kernels  204 us (99%)
  local copies, waits for them, and re-layouts  2.64 us (1%)
    pallas_call x1, Pallas kernels, body(): pl.pallas_call(functools.partial(kernel, experts), out_shape=[jax.ShapeDt...  204 us

profile of v2, /device:TPU:1, one launch (start us, length us, event | category | flops | bytes accessed | tf_op | source)
XLA Modules:
  0.0 207.0 jit_solution(13809296693056016966)
XLA Ops:
  0.6 203.7 %relay_layer.1 = (bf16[64,3584]{1,0:T(8,128)(2,1)}, bf16[64,3584]{1,0:T(8,128)(2,1)}) custom-call(bf16[64,3584]{1,0:T(8,128)(2,1)} %bitcast.17, s32[1,64]{1,0:T(1,128)} %bitcast.20, f32[1,64]{1,0:T(1,128)} %bitcast.21, bf16[64,3584]{1,0:T(8,128)(2,1)} %bitcast.18, bf16[64,3584]{1,0:T(8,128)(2,1)} %bitcast.19, s32[1,64]{1,0:T(1,128)} %bitcast.22, ...), custom_call_target="tpu_custom_call" | custom-call | tf_op jit(solution)/shard_map/relay_layer/pallas_call | solution.py:658
  204.4 0.0 copy-start
  204.4 1.9 copy.15
  206.3 0.0 copy-done
  206.3 0.8 copy.16
Async XLA Ops:
  204.4 1.9 copy-start

commit v3 on v2

--- a/solution.py
+++ b/solution.py
@@ -169,6 +169,8 @@
     for copy in kept:
         copy.start()
 
+    for copy in kept:
+        copy.wait()
     pl.semaphore_wait(barrier, 2 * experts + 4)
 
     units = w_down.shape[0] - DETOUR
@@ -181,7 +183,7 @@
     def detour(which, step):
         if which == 2:
             stops = (
-                w_down.at[pl.ds(units, DETOUR)],
+                down_w.at[0, pl.ds(units, DETOUR)],
                 passing_w.at[0],
                 passing_w.at[1],
                 down_w.at[1, pl.ds(units, DETOUR)],
@@ -207,9 +209,9 @@
 
     detour(2, 0).start()
     swaps = (
-        (w_gate, gate_w.at[1]),
-        (w_up, up_w.at[1]),
-        (w_down.at[pl.ds(0, units)], down_w.at[1, pl.ds(0, units)]),
+        (gate_w.at[0], gate_w.at[1]),
+        (up_w.at[0], up_w.at[1]),
+        (down_w.at[0, pl.ds(0, units)], down_w.at[1, pl.ds(0, units)]),
     )
     swapped = [
         send(src, dst, w_send, i, w_recv, i, (section, y, z_weights, c))
@@ -221,31 +223,32 @@
     def normalized(ref, slot):
         wide = ref[...].astype(F32)
         inverse = lax.rsqrt(jnp.mean(wide * wide, axis=-1, keepdims=True) + 1e-06)
-        staged[slot] = (wide * inverse * gain[...]).astype(BF16)
+        staged[slot * tokens : (slot + 1) * tokens] = (wide * inverse * gain[...]).astype(BF16)
         return inverse
 
     normalized(fwd_act, 0)
     bwd_inverse = normalized(bwd_act, 1)
-    staged[2] = (as_column(bwd_gate[...]) * bwd_grad[...].astype(F32)).astype(BF16)
+    staged[2 * tokens :] = (as_column(bwd_gate[...]) * bwd_grad[...].astype(F32)).astype(BF16)
 
     fwd_slots = slot_numbers(fwd_route[...])
     bwd_slots = slot_numbers(bwd_route[...])
 
-    def placing(slots, offset):
-        target = (slots[2] * SLAB + slots[3]).astype(jnp.int32) + offset
-        return selector(iota((experts * SLAB, tokens), 0) == target)
-
-    place_fwd = placing(fwd_slots, 0)
-    place_bwd = placing(bwd_slots, CAP)
-    place_grad = placing(bwd_slots, 2 * CAP)
+    detour(2, 0).wait_recv()
+    detour(2, 1).start()
+
+    def targets(slots, offset):
+        return slots[2] * SLAB + slots[3] + offset
+
+    target = jnp.concatenate(
+        [targets(fwd_slots, 0), targets(bwd_slots, CAP), targets(bwd_slots, 2 * CAP)], axis=1
+    ).astype(jnp.int32)
+    place = selector(iota((experts * SLAB, 3 * tokens), 0) == target)
 
     def place_half(k, _):
         def place_tile(i, _):
             source = aligned(k * half + i * tile, tile)
-            placed = dot(place_fwd, staged[0, :, source])
-            placed += dot(place_bwd, staged[1, :, source])
-            placed += dot(place_grad, staged[2, :, source])
-            outgoing[k, :, aligned(i * tile, tile)] = placed.astype(BF16)
+            placed = dot(place, staged[:, source]).astype(BF16)
+            outgoing[k, :, aligned(i * tile, tile)] = placed
             return 0
 
         return lax.fori_loop(0, tiles, place_tile, 0)
@@ -261,7 +264,7 @@
             outgoing.at[k, slab(there)],
             near.at[slab(me)],
             a_send,
-            step * 2 + k,
+            0,
             a_recv,
             me,
             (section, there, z, k),
@@ -276,8 +279,6 @@
     stay.start()
     dispatch(0, core).start()
     lax.fori_loop(1, experts, dispatch_row, 0)
-    detour(2, 0).wait_recv()
-    detour(2, 1).start()
 
     def arrival(index):
         return send(
@@ -295,9 +296,9 @@
             near.at[slab(index)],
             far.at[slab(index)],
             f_send,
-            index,
+            0,
             f_recv,
-            index,
+            0,
             (section, y, z_rows, c),
         )
 
@@ -338,33 +339,37 @@
     detour(2, 1).wait_recv()
     detour(2, 2).start()
 
-    def far_arrived(index, _):
-        forward(index).wait_recv()
-        return 0
-
-    lax.fori_loop(0, slabs, far_arrived, 0)
-    take_apart(far, block)
-
-    def first_products(b):
+    def part_of(group):
+        return pl.ds(group * block, block)
+
+    def first_products(b, group):
+        part = part_of(group)
+
         def of_rows(kind, _):
             for which, weight in ((0, gate_w), (1, up_w)):
-                product = dot(rows[kind], weight[b])
-                pre[b, 2 * kind + which] = product
-                pre_out[b, 2 * kind + which] = product.astype(BF16)
+                product = dot(rows[kind, part], weight[b])
+                pre[b, 2 * kind + which, part] = product
+                pre_out[b, 2 * kind + which, part] = product.astype(BF16)
             return 0
 
         lax.fori_loop(0, 2, of_rows, 0)
 
-    def down_product(b):
-        product = dot_nt(rows[2], down_w[b])
-        pre[b, 4] = product
-        pre_out[b, 4] = product.astype(BF16)
-
-    def cross(b, first, count, index):
-        part = pl.ds(first, count)
+    def down_product(b, part):
+        product = dot_nt(rows[2, part], down_w[b])
+        pre[b, 4, part] = product
+        pre_out[b, 4, part] = product.astype(BF16)
+
+    def cross(index):
+        b, values, part = (
+            (0, pl.ds(0, 5), part_of(0)),
+            (1, pl.ds(0, 4), part_of(0)),
+            (0, pl.ds(0, 5), part_of(1)),
+            (1, pl.ds(0, 4), part_of(1)),
+            (1, pl.ds(4, 1), pl.ds(0, 2 * block)),
+        )[index]
         return send(
-            pre_out.at[b, part],
-            pre_in.at[b, part],
+            pre_out.at[b, values, part],
+            pre_in.at[b, values, part],
             c_send,
             index,
             c_recv,
@@ -372,41 +377,53 @@
             (section, y, z, core),
         )
 
-    def activate(b):
-        gate_pre = pre[b, 0] + pre_in[b, 0].astype(F32)
-        up_pre = pre[b, 1] + pre_in[b, 1].astype(F32)
-        hidden[b, 0] = (gate_pre * jax.nn.sigmoid(gate_pre) * up_pre).astype(BF16)
-
-    def derive(b):
-        gate_pre = pre[b, 2] + pre_in[b, 2].astype(F32)
-        up_pre = pre[b, 3] + pre_in[b, 3].astype(F32)
-        grad = pre[b, 4] + pre_in[b, 4].astype(F32)
+    def crossed(b, which, part):
+        return pre[b, which, part] + pre_in[b, which, part].astype(F32)
+
+    def activate(b, part):
+        gate_pre = crossed(b, 0, part)
+        hidden[b, 0, part] = (
+            gate_pre * jax.nn.sigmoid(gate_pre) * crossed(b, 1, part)
+        ).astype(BF16)
+
+    def derive(b, part):
+        gate_pre = crossed(b, 2, part)
+        up_pre = crossed(b, 3, part)
+        grad = crossed(b, 4, part)
         logistic = jax.nn.sigmoid(gate_pre)
-        hidden[b, 1] = (
+        hidden[b, 1, part] = (
             grad * up_pre * logistic * (1.0 + gate_pre * (1.0 - logistic))
         ).astype(BF16)
-        hidden[b, 2] = (grad * gate_pre * logistic).astype(BF16)
-
-    for copy in kept:
-        copy.wait()
-    first_products(0)
-    down_product(0)
-    cross(0, 0, 5, 0).start()
-
-    swapped[0].wait_recv()
-    swapped[1].wait_recv()
-    first_products(1)
-    cross(1, 0, 4, 1).start()
-    cross(0, 0, 5, 0).wait_recv()
-    activate(0)
-    derive(0)
-    cross(1, 0, 4, 1).wait_recv()
-    activate(1)
-
+        hidden[b, 2, part] = (grad * gate_pre * logistic).astype(BF16)
+
+    def process(group):
+        part = part_of(group)
+        first_products(0, group)
+        down_product(0, part)
+        cross(2 * group).start()
+        if group == 0:
+            swapped[0].wait_recv()
+            swapped[1].wait_recv()
+        first_products(1, group)
+        cross(2 * group + 1).start()
+        cross(2 * group).wait_recv()
+        activate(0, part)
+        derive(0, part)
+        cross(2 * group + 1).wait_recv()
+        activate(1, part)
+
+    process(0)
+
+    forwarded = send(near, far, f_send, 0, f_recv, 0, (section, y, z_rows, c))
+    forwarded.wait_recv()
+    take_apart(far, block)
+    process(1)
+
+    everything = pl.ds(0, 2 * block)
     swapped[2].wait_recv()
     detour(2, 2).wait_recv()
-    down_product(1)
-    cross(1, 4, 1, 2).start()
+    down_product(1, everything)
+    cross(4).start()
 
     def give_back(which, piece):
         columns = piece_columns(piece)
@@ -427,6 +444,9 @@
                 detour(which, 0).start()
             else:
                 give_back(which, piece).start()
+            if which == 1 and piece == 0:
+                detour(0, 0).wait_recv()
+                detour(0, 1).start()
 
     def split(which, columns, values):
         own[which, :, columns] = values[:block]
@@ -443,8 +463,8 @@
 
     give_back_all(0, forward_tile)
 
-    cross(1, 4, 1, 2).wait_recv()
-    derive(1)
+    cross(4).wait_recv()
+    derive(1, everything)
 
     def backward_tile(i, _):
         columns = aligned(i * tile, tile)
@@ -472,10 +492,10 @@
         return send(
             y_out.at[which, slots_of(there * 2 + to_core), columns],
             y_in.at[which, c, slots_of(y), columns],
-            y_send.at[which, piece],
-            step * 2 + to_core,
-            y_recv.at[which, piece],
-            y * 2 + c,
+            y_send,
+            which,
+            y_recv.at[which],
+            piece,
             (section, there, z, to_core),
         )
 
@@ -511,42 +531,27 @@
         returning(which, piece, 0, core).start()
         lax.fori_loop(1, experts, return_row, 0)
 
-    def returned(which, piece, k, e):
-        columns = piece_columns(piece)
-        return send(
-            y_out.at[which, slots_of(0), columns],
-            y_in.at[which, k, slots_of(e), columns],
-            y_send.at[which, piece],
-            0,
-            y_recv.at[which, piece],
-            e * 2 + k,
-            (section, y, z, core),
-        )
+    others = pl.ds(0, (slabs - 1) * BACK)
 
     def collect(which, piece):
-        def from_row(step, _):
-            there = y_at(step, -1)
-            returned(which, piece, 0, there).wait_recv()
-            returned(which, piece, 1, there).wait_recv()
-            return 0
-
         staying(which, piece).wait()
-        returned(which, piece, core, y).wait_recv()
-        lax.fori_loop(1, experts, from_row, 0)
-
-    detour(0, 0).wait_recv()
-    detour(0, 1).start()
+        part = y_out.at[which, others, piece_columns(piece)]
+        send(
+            part, part, y_send, which, y_recv.at[which], piece, (section, y, z, core)
+        ).wait_recv()
+
     detour(1, 0).wait_recv()
     detour(1, 1).start()
     send_back(0, 1)
     detour(0, 1).wait_recv()
     detour(0, 2).start()
+    detour(1, 1).wait_recv()
+    detour(1, 2).start()
     send_back(0, 2)
     send_back(0, 0)
-    detour(1, 1).wait_recv()
-    detour(1, 2).start()
-    for piece in range(len(pieces)):
-        send_back(1, piece)
+    send_back(1, 1)
+    send_back(1, 0)
+    send_back(1, 2)
 
     def picking(slots):
         target = (slots[0] * BACK + slots[1]).astype(jnp.int32)
@@ -573,7 +578,8 @@
 
     pick_bwd = picking(bwd_slots)
     dotted = jnp.zeros((tokens, tile), F32)
-    for piece, (start, count) in enumerate(pieces):
+    for piece in (1, 0, 2):
+        start, count = pieces[piece]
         collect(1, piece)
         for k in range(2):
 
@@ -605,31 +611,18 @@
     for which in range(3):
         for step in range(3):
             detour(which, step).wait_send()
-    dispatch(0, core).wait_send()
     for which in range(2):
-        for piece in range(len(pieces)):
-            returning(which, piece, 0, core).wait_send()
-            if piece:
-                give_back(which, piece).wait_send()
-
-    def row_left(step, _):
-        for k in range(2):
-            dispatch(step, k).wait_send()
-            for which in range(2):
-                for piece in range(len(pieces)):
-                    returning(which, piece, step, k).wait_send()
-        return 0
-
-    lax.fori_loop(1, experts, row_left, 0)
-
-    def forward_left(index, _):
-        forward(index).wait_send()
-        return 0
-
-    lax.fori_loop(0, slabs, forward_left, 0)
-    cross(0, 0, 5, 0).wait_send()
-    cross(1, 0, 4, 1).wait_send()
-    cross(1, 4, 1, 2).wait_send()
+        part = y_out.at[which, others]
+        send(
+            part, part, y_send, which, y_recv.at[which], 0, (section, y, z, core)
+        ).wait_send()
+        for piece in range(1, len(pieces)):
+            give_back(which, piece).wait_send()
+    part = near.at[pl.ds(0, (slabs - 1) * SLAB)]
+    send(part, part, a_send, 0, a_recv, 0, (section, y, z, core)).wait_send()
+    forwarded.wait_send()
+    for index in range(5):
+        cross(index).wait_send()
     to_next.wait()
     to_previous.wait()
 
@@ -661,7 +654,7 @@
         in_specs=[vmem] * 8 + [anywhere] * 3,
         out_specs=[vmem] * 2,
         scratch_shapes=[
-            pltpu.VMEM((3, tokens, width), BF16),
+            pltpu.VMEM((3 * tokens, width), BF16),
             pltpu.VMEM((2, experts * SLAB, half), BF16),
             pltpu.VMEM((slabs * SLAB, half), BF16),
             pltpu.VMEM((slabs * SLAB, half), BF16),
@@ -685,16 +678,16 @@
             dma((4 + 2 * len(PIECES),)),
             dma((3,)),
             dma((3,)),
+            dma((1,)),
             dma((slabs,)),
-            dma((slabs,)),
-            dma((slabs,)),
-            dma((slabs,)),
-            dma((3,)),
-            dma((3,)),
+            dma((1,)),
+            dma((1,)),
+            dma((5,)),
+            dma((5,)),
             dma((2, len(PIECES))),
             dma((2, len(PIECES))),
-            dma((2, len(PIECES), slabs)),
-            dma((2, len(PIECES), slabs)),
+            dma((2,)),
+            dma((2, len(PIECES))),
             dma((2,)),
             dma((2,)),
             dma((9,)),

time: 207 us -> 206 us (level)
  no operation moved by 1% of the time
where the time goes in v3:
time: 206 us
  Pallas kernels  202 us (98%)
  local copies, waits for them, and re-layouts  2.64 us (1%)
    pallas_call x1, Pallas kernels, body(): pl.pallas_call(functools.partial(kernel, experts), out_shape=[jax.ShapeDt...  202 us

profile of v3, /device:TPU:1, one launch (start us, length us, event | category | flops | bytes accessed | tf_op | source)
XLA Modules:
  0.0 205.6 jit_solution(9333503012540728362)
XLA Ops:
  0.6 202.3 %relay_layer.1 = (bf16[64,3584]{1,0:T(8,128)(2,1)}, bf16[64,3584]{1,0:T(8,128)(2,1)}) custom-call(bf16[64,3584]{1,0:T(8,128)(2,1)} %bitcast.17, s32[1,64]{1,0:T(1,128)} %bitcast.20, f32[1,64]{1,0:T(1,128)} %bitcast.21, bf16[64,3584]{1,0:T(8,128)(2,1)} %bitcast.18, bf16[64,3584]{1,0:T(8,128)(2,1)} %bitcast.19, s32[1,64]{1,0:T(1,128)} %bitcast.22, ...), custom_call_target="tpu_custom_call" | custom-call | tf_op jit(solution)/shard_map/relay_layer/pallas_call | solution.py:651
  202.9 0.0 copy-start
  202.9 1.9 copy.15
  204.8 0.0 copy-done
  204.8 0.8 copy.16
Async XLA Ops:
  202.9 1.9 copy-start
